TPU v7x, 128 devices: a whole 4x4x4 slice. The times are simulated.
128 devices in a mesh: dp: 32 (over z, x, core), head: 4 (over y).
Axes of the slice: x: 4, y: 4, z: 4, core: 2. Of those that a mesh axis runs over, the one named last changes fastest.
Arguments:
- hidden: bfloat16 [1024, 2048], P('dp'), may hold values from -6 to 6
- attn_gain: float32 [2048], replicated, may hold values from 0.1 to 1.9
- w_query: bfloat16 [2048, 3072], P(None, 'head'), may hold values from -0.125 to 0.125
- w_latent: bfloat16 [2048, 576], P(None, 'head'), may hold values from -0.125 to 0.125
- latent_gain: float32 [512], replicated, may hold values from 0.1 to 1.9
- w_key_up: bfloat16 [16, 128, 512], P('head'), may hold values from -0.5 to 0.5
- w_value_up: bfloat16 [16, 512, 128], P('head'), may hold values from -0.25 to 0.25
- w_out: bfloat16 [2048, 2048], P('head'), may hold values from -0.125 to 0.125
- kv_cache: bfloat16 [1024, 128, 576], P('dp'), may hold values from -110 to 110
- lengths: int32 [1024], P('dp'), may hold values from 1 to 128, 65536 in all
- live_mask: int32 [1024], P('dp'), may hold values 0 or 1
- mlp_gain: float32 [2048], replicated, may hold values from 0.1 to 1.9
- w_router: bfloat16 [2048, 64], replicated, may hold values from -0.125 to 0.125
- routes: int32 [1024, 6], P('dp'), may hold values from 0 to 63, all different within a row; in each aligned block of 32 rows (0 to 31, 32 to 63, ...) at most 6 rows name the same one
- w_experts_in: bfloat16 [64, 2048, 2, 1408], P('dp', None, None, 'head'), may hold values from -0.125 to 0.125
- w_experts_out: bfloat16 [64, 1408, 2048], P('dp', 'head'), may hold values from -0.15625 to 0.15625
- w_shared_in: bfloat16 [2048, 2, 1408], P(None, None, 'head'), may hold values from -0.125 to 0.125
- w_shared_out: bfloat16 [1408, 2048], P('head'), may hold values from -0.15625 to 0.15625
Outputs:
- output: bfloat16 [1024, 2048], P('dp', 'head')
Inputs may be any that keep to these rules, and one draw needn't show every extreme that they name: Among the routes of one device's 32 rows no expert is named more than 6 times, a bound that some block reaches. Request t has cached positions 0 to lengths[t] - 1; some request has 128.
All inputs are finite; a program needn't handle non-finite values. No bound on the sum of `lengths` or of `live_mask` on one device may be relied on, other than what follows from the above.
Results may differ from a plain program's by a relative error of at most 0.02.
The roundings to bfloat16 on the way count: a program that leaves them out, or rounds other values in their place, can miss the bound.
Values may be sent and summed in bfloat16 or wider, within the bound.
A program may use at most 128 MiB of HBM per device.

v0:
```python
import math
import jax
import jax.numpy as jnp
from jax import lax
from jax.sharding import PartitionSpec as P

NOPE = 128
ROPE = 64
VDIM = 128
LAT = 512
norm_eps = 1e-06
rope_theta = 50000.0
route_scale = 2.446


def rms_norm(values, weights):
    mean_square = jnp.mean(values * values, axis=-1, keepdims=True)
    return values * lax.rsqrt(mean_square + norm_eps) * weights


def rotary(values, positions):
    half_size = values.shape[-1] // 2
    frequency = rope_theta ** (-jnp.arange(half_size, dtype=jnp.float32) / half_size)
    angles = positions.reshape((-1,) + (1,) * (values.ndim - 1)) * frequency
    first_half = values[..., :half_size]
    second_half = values[..., half_size:]
    cosine = jnp.cos(angles)
    sine_part = jnp.sin(angles)
    return jnp.concatenate(
        [
            first_half * cosine - second_half * sine_part,
            second_half * cosine + first_half * sine_part,
        ],
        axis=-1,
    )


def body(
    hidden,
    attn_gain,
    w_query,
    w_latent,
    latent_gain,
    w_key_up,
    w_value_up,
    w_out,
    kv_cache,
    lengths,
    live_mask,
    mlp_gain,
    w_router,
    routes,
    w_experts_in,
    w_experts_out,
    w_shared_in,
    w_shared_out,
):
    request_count = hidden.shape[0]
    model_width = hidden.shape[1]
    local_heads = w_key_up.shape[0]
    cache_length = kv_cache.shape[1]
    head_count = lax.axis_size("head")
    share_width = model_width // head_count
    column_start = lax.axis_index("head") * share_width
    dp_count = lax.axis_size("dp")
    local_experts = w_experts_in.shape[0]
    expert_total = local_experts * dp_count
    top_count = routes.shape[1]
    capacity = max(2, 2 * top_count * request_count // expert_total)
    normed = rms_norm(hidden.astype(jnp.float32), attn_gain).astype(jnp.bfloat16)
    query_all = jnp.dot(normed, w_query, preferred_element_type=jnp.float32).reshape(
        request_count, local_heads, NOPE + ROPE
    )
    positions = lengths.astype(jnp.float32)
    query_nope = query_all[..., :NOPE].astype(jnp.bfloat16)
    query_rope = rotary(query_all[..., NOPE:], positions).astype(jnp.bfloat16)
    query_latent = jnp.einsum(
        "rhn,hnc->rhc", query_nope, w_key_up, preferred_element_type=jnp.float32
    ).astype(jnp.bfloat16)
    fresh_part = jnp.dot(normed, w_latent, preferred_element_type=jnp.float32).astype(jnp.bfloat16)
    fresh_kv = lax.all_gather(fresh_part, "head", axis=1, tiled=True)
    latent_new = rms_norm(fresh_kv[:, :LAT].astype(jnp.float32), latent_gain)
    rope_new = rotary(fresh_kv[:, LAT:].astype(jnp.float32), positions)
    key_new = jnp.concatenate([latent_new, rope_new], axis=-1).astype(jnp.bfloat16)
    query_full = jnp.concatenate([query_latent, query_rope], axis=-1)
    inverse_root = 1.0 / math.sqrt(NOPE + ROPE)
    scores = (
        jnp.einsum("rhc,rjc->rhj", query_full, kv_cache, preferred_element_type=jnp.float32)
        * inverse_root
    )
    in_cache = jnp.arange(cache_length, dtype=jnp.int32)[None, :] < lengths[:, None]
    scores = jnp.where(in_cache[:, None, :], scores, -jnp.inf)
    score_new = (
        jnp.einsum("rhc,rc->rh", query_full, key_new, preferred_element_type=jnp.float32)
        * inverse_root
    )
    highest = jnp.maximum(jnp.max(scores, axis=-1), score_new)
    weights_cached = jnp.exp(scores - highest[..., None])
    weight_new = jnp.exp(score_new - highest)
    denominator = jnp.sum(weights_cached, axis=-1) + weight_new
    probabilities = (weights_cached / denominator[..., None]).astype(jnp.bfloat16)
    prob_new = (weight_new / denominator).astype(jnp.bfloat16)
    context = jnp.einsum(
        "rhj,rjc->rhc", probabilities, kv_cache[..., :LAT], preferred_element_type=jnp.float32
    )
    context = (
        context
        + prob_new.astype(jnp.float32)[..., None] * key_new[:, None, :LAT].astype(jnp.float32)
    ).astype(jnp.bfloat16)
    values = jnp.einsum(
        "rhc,hcv->rhv", context, w_value_up, preferred_element_type=jnp.float32
    ).astype(jnp.bfloat16)
    partial_value = jnp.dot(
        values.reshape(request_count, local_heads * VDIM), w_out, preferred_element_type=jnp.float32
    )
    attention = lax.psum(partial_value.astype(jnp.bfloat16), "head").astype(jnp.float32)
    mixed_rows = (hidden.astype(jnp.float32) + attention).astype(jnp.bfloat16)
    ffn_input = rms_norm(mixed_rows.astype(jnp.float32), mlp_gain).astype(jnp.bfloat16)
    mixed_share = lax.dynamic_slice_in_dim(mixed_rows, column_start, share_width, 1)
    logits = jnp.dot(ffn_input, w_router, preferred_element_type=jnp.float32)
    chosen = jax.nn.sigmoid(jnp.take_along_axis(logits, routes, axis=1))
    route_weight = (
        route_scale
        * live_mask.astype(jnp.float32)[:, None]
        * chosen
        / jnp.sum(chosen, axis=1, keepdims=True)
    )
    pair_count = request_count * top_count
    flat_routes = routes.reshape(pair_count)
    live_pairs = jnp.repeat(live_mask, top_count)
    member = (
        (flat_routes[:, None] == jnp.arange(expert_total, dtype=jnp.int32)[None, :])
        & (live_pairs[:, None] == 1)
    ).astype(jnp.int32)
    earlier = jnp.cumsum(member, axis=0) - member
    slot_rank = jnp.sum(earlier * member, axis=1)
    slot_total = expert_total * capacity
    buffer_slot = jnp.where(live_pairs == 1, flat_routes * capacity + slot_rank, slot_total)
    token_of_pair = jnp.arange(pair_count, dtype=jnp.int32) // top_count
    spread = ffn_input[token_of_pair]
    packed = (
        jnp.zeros((slot_total, ffn_input.shape[1]), jnp.bfloat16)
        .at[buffer_slot]
        .set(spread, mode="drop")
    )
    arrived = lax.all_to_all(
        packed.reshape(dp_count, local_experts, capacity, ffn_input.shape[1]),
        "dp",
        split_axis=0,
        concat_axis=0,
        tiled=True,
    )
    gate_up = jnp.einsum(
        "secd,edkf->seckf", arrived, w_experts_in, preferred_element_type=jnp.float32
    )
    acting = (jax.nn.silu(gate_up[..., 0, :]) * gate_up[..., 1, :]).astype(jnp.bfloat16)
    expert_part = jnp.einsum(
        "secf,efd->secd", acting, w_experts_out, preferred_element_type=jnp.float32
    )
    expert_share = lax.psum_scatter(
        expert_part.astype(jnp.bfloat16), "head", scatter_dimension=3, tiled=True
    )
    returned = lax.all_to_all(expert_share, "dp", split_axis=0, concat_axis=0, tiled=True)
    returned_rows = returned.reshape(slot_total, share_width)
    pick_slot = jnp.minimum(buffer_slot, slot_total - 1)
    pair_rows = returned_rows[pick_slot].astype(jnp.float32)
    routed = jnp.sum(
        (route_weight.reshape(pair_count)[:, None] * pair_rows).reshape(
            request_count, top_count, share_width
        ),
        axis=1,
    )
    shared_width = w_shared_out.shape[0]
    shared_pair = jnp.dot(
        ffn_input,
        w_shared_in.reshape(model_width, 2 * shared_width),
        preferred_element_type=jnp.float32,
    ).reshape(request_count, 2, shared_width)
    shared_act = (jax.nn.silu(shared_pair[:, 0]) * shared_pair[:, 1]).astype(jnp.bfloat16)
    shared_part = jnp.dot(shared_act, w_shared_out, preferred_element_type=jnp.float32)
    shared_share = lax.psum_scatter(
        shared_part.astype(jnp.bfloat16), "head", scatter_dimension=1, tiled=True
    ).astype(jnp.float32)
    return (mixed_share.astype(jnp.float32) + shared_share + routed).astype(jnp.bfloat16)


def solution(mesh):
    placed = (
        P("dp", None),
        P(),
        P(None, "head"),
        P(None, "head"),
        P(),
        P("head", None, None),
        P("head", None, None),
        P("head", None),
        P("dp", None, None),
        P("dp"),
        P("dp"),
        P(),
        P(),
        P("dp", None),
        P("dp", None, None, "head"),
        P("dp", "head", None),
        P(None, None, "head"),
        P("head", None),
    )
    return jax.shard_map(
        body, mesh=mesh, in_specs=placed, out_specs=P("dp", "head"), check_vma=False
    )
```

profile of v0, /device:TPU:1, one launch (start us, length us, event | category | flops | bytes accessed | tf_op | source)
XLA Modules:
  0.0 187.7 jit_solution(8351223471823655975)
XLA Ops:
  6.6 0.8 convert_element_type.107
  7.4 0.9 iota_compare_fusion.2
  8.2 1.0 fusion.40
  9.3 1.5 fusion.29
  10.8 10.4 %all-gather = bf16[4,144,32]{1,2,0:T(8,128)(2,1)S(1)} all-gather(bf16[1,144,32]{1,2,0:T(8,128)(2,1)S(1)} %fusion.29), channel_id=1, replica_groups=mesh['dp'=32,'head'=4] {'head'}, dimensions={0}, use_global_device_ids=true | all-gather | bytes 46080 | tf_op jit(solution)/shard_map/all_gather | solution.py:81
  21.2 0.1 reshape.357
  21.3 0.1 fusion.50
  21.5 1.6 fusion.61
  23.0 0.1 reshape.311
  23.2 0.1 fusion.77
  23.3 0.1 fusion.75
  23.4 1.2 fusion.26
  24.7 0.1 subtract_convert_fusion.1
  24.8 0.1 maximum_bitcast_fusion
  24.9 0.1 pad_maximum_fusion
  25.0 0.3 fusion.46
  25.3 3.4 %fusion.78 = (f32[32,4]{1,0:T(8,128)S(1)}, f32[32,4,128]{2,1,0:T(4,128)S(1)}) fusion(bf16[32,128,576]{1,2,0:T(8,128)(2,1)} %param.26, bf16[32,4,576]{2,0,1:T(8,128)(2,1)S(1)} %pad_maximum_fusion, pred[32,128]{1,0:T(8,128)(4,1)S(1)} %iota_compare_fusion.2), kind=kOutput, calls=%fused_computation.128 | convolution fusion | flops 18923392 | bytes 4936192 | tf_op jit(solution)/shard_map/rhc,rjc->rhj/dot_general | solution.py:88
  28.7 0.2 fusion.57
  28.9 0.1 copy-done.1
  29.1 1.2 fusion.23
  30.3 0.2 fusion.28
  30.6 0.3 copy-done.3
  30.8 1.1 convolution_convert_fusion.1
  32.1 0.1 broadcast_in_dim.27
  32.1 0.1 eq.62
  32.2 0.1 eq.57
  32.4 0.1 copy.93
  32.5 0.1 copy.92
  32.6 0.1 mul.265
  32.7 0.1 eq.58
  32.8 0.6 reduce-window.6
  33.4 0.2 slice_reduce_fusion
  33.7 0.1 bitcast_bitcast_fusion
  33.8 41.9 %all-reduce.3.cloned.1.call-done = bf16[32,2048]{1,0:T(8,128)(2,1)} async-done(((bf16[32,2048]{1,0:T(8,128)(2,1)}), bf16[32,2048]{1,0:T(8,128)(2,1)}) %all-reduce.3.cloned.1.call-update) | async-done | bytes 131088 | tf_op jit(solution)/shard_map/psum | solution.py:116
  75.7 1.1 fusion.37
  76.8 0.6 copy-done.5
  77.4 0.1 fusion.39
  77.5 5.6 %scatter_custom_fusion = bf16[384,2048]{1,0:T(8,128)(2,1)} fusion(s32[192]{0:T(256)S(1)} %bitcast.114, bf16[32,2048]{1,0:T(8,128)(2,1)S(1)} %fusion.39, s32[1024]{0:T(1024)S(1)} %pad_clamp_fusion.1, bf16[]{:T(256)} %constant.75.clone.1), kind=kCustom, calls=%fused_computation.28 | custom fusion | bytes 1572866 | tf_op jit(solution)/shard_map/scatter | solution.py:144
  83.1 3.7 %reshape.317 = bf16[32,2,6,2048]{3,2,1,0:T(8,128)(2,1)} reshape(bf16[384,2048]{1,0:T(8,128)(2,1)} %scatter_custom_fusion) | data formatting | bytes 3145728 | tf_op jit(solution)/shard_map/reshape | solution.py:147
  86.8 3.2 %copy.96 = bf16[32,2,6,2048]{3,1,2,0:T(2,128)(2,1)S(1)} copy(bf16[32,2,6,2048]{3,2,1,0:T(8,128)(2,1)} %reshape.317) | data formatting | bytes 3145728 | tf_op jit(solution)/shard_map/reshape | solution.py:147
  90.0 32.3 %all_to_all.10 = bf16[32,2,6,2048]{3,1,2,0:T(2,128)(2,1)S(1)} all-to-all(bf16[32,2,6,2048]{3,1,2,0:T(2,128)(2,1)S(1)} %copy.96), channel_id=1, replica_groups=mesh['dp'=32,'head'=4] {'dp'}, dimensions={0} | all-to-all | bytes 3145728 | tf_op jit(solution)/shard_map/all_to_all | solution.py:146
  122.4 5.9 %fusion.15 = f32[32,2,6,2,352]{4,0,3,2,1:T(8,128)S(1)} fusion(bf16[2,2048,2,352]{1,3,2,0:T(8,128)(2,1)} %param.32, bf16[32,2,6,2048,1]{3,1,2,0,4:T(2,128)(2,1)S(1)} %bitcast.106), kind=kOutput, calls=%fused_computation.17 | convolution fusion | flops 1107296256 | bytes 8421376 | tf_op jit(solution)/shard_map/secd,edkf->seckf/dot_general | solution.py:153
  128.3 2.2 %fusion.11 = bf16[32,2,6,2048]{3,0,2,1:T(8,128)(2,1)} fusion(bf16[2,352,2048]{2,1,0:T(8,128)(2,1)S(1)} %copy-done.10, f32[32,2,6,2,352]{4,0,3,2,1:T(8,128)S(1)} %fusion.15), kind=kOutput, calls=%fused_computation.13 | convolution fusion | flops 555245568 | bytes 5537792 | tf_op jit(solution)/shard_map/secf,efd->secd/dot_general | solution.py:157
  130.5 0.1 copy.89
  130.6 0.1 reshape.337
  130.7 0.6 pad_clamp_fusion
  131.3 1.1 fusion.79
  132.4 1.6 gather_fusion.1
  134.1 0.1 reshape.340
  134.2 0.1 copy.90
  134.3 2.9 %fusion.6 = f32[32,2,352]{2,0,1:T(8,128)S(1)} fusion(bf16[2048,2,352]{0,2,1:T(8,128)(2,1)} %param.34, bf16[32,2048]{1,0:T(8,128)(2,1)S(1)} %fusion.39), kind=kOutput, calls=%fused_computation.10 | convolution fusion | flops 92274688 | bytes 3104768 | tf_op jit(solution)/shard_map/dot_general | solution.py:174
  137.2 1.0 convolution_convert_fusion
  138.3 13.7 %reduce-scatter.5.cloned.1.call-done = bf16[32,2,6,512]{3,0,2,1:T(8,128)(2,1)} async-done(((bf16[32,2,6,2048]{3,0,2,1:T(8,128)(2,1)}), bf16[32,2,6,512]{3,0,2,1:T(8,128)(2,1)}) %reduce-scatter.5.cloned.1.call-update) | async-done | bytes 393232 | tf_op jit(solution)/shard_map/reduce_scatter | solution.py:160
  151.9 2.1 %copy.99 = bf16[32,2,6,512]{3,1,2,0:T(2,128)(2,1)} copy(bf16[32,2,6,512]{3,0,2,1:T(8,128)(2,1)} %reduce-scatter.5.cloned.1.call-done) | data formatting | bytes 786432 | tf_op jit(solution)/shard_map/reduce_scatter | solution.py:160
  154.1 8.6 %all-to-all-start.1 = ((bf16[32,2,6,512]{3,1,2,0:T(2,128)(2,1)}), bf16[32,2,6,512]{3,1,2,0:T(2,128)(2,1)S(1)}, u32[]{:S(2)}, u32[]{:S(2)}) async-start(bf16[32,2,6,512]{3,1,2,0:T(2,128)(2,1)} %copy.99), calls=%async_computation.3 | async-start | bytes 786432 | tf_op jit(solution)/shard_map/all_to_all | solution.py:163
  162.7 0.6 multiply_divide_fusion
  163.3 0.8 copy.91
  164.0 8.8 %all-to-all-done.1 = bf16[32,2,6,512]{3,1,2,0:T(2,128)(2,1)S(1)} async-done(((bf16[32,2,6,512]{3,1,2,0:T(2,128)(2,1)}), bf16[32,2,6,512]{3,1,2,0:T(2,128)(2,1)S(1)}, u32[]{:S(2)}, u32[]{:S(2)}) %all-to-all-start.1) | async-done | bytes 393248 | tf_op jit(solution)/shard_map/all_to_all | solution.py:163
  172.8 0.9 copy.100
  173.7 1.2 reshape.318
  174.9 1.8 gather_fusion
  176.7 1.8 reshape.320
  178.4 1.3 multiply_reduce_fusion
  179.7 1.4 add_convert_fusion
  (51 shorter events, 0.6 us)
Async XLA Ops:
  6.5 14.9 %copy-start = (bf16[2048,768]{1,0:T(8,128)(2,1)S(1)}, bf16[2048,768]{1,0:T(8,128)(2,1)}, u32[]{:S(2)}) copy-start(bf16[2048,768]{1,0:T(8,128)(2,1)} %param.20) | copy-start | bytes 9437188
  6.5 69.2 %all-reduce.3.cloned.1.call-start = ((), (), s32[]{:S(2)}) async-start(), calls=%async_computation.4 | async-start | bytes 262144 | tf_op jit(solution)/shard_map/psum | solution.py:116
  21.2 2.2 %copy-start.9 = (f32[512]{0:T(512)S(1)}, f32[512]{0:T(512)}, u32[]{:S(2)}) copy-start(f32[512]{0:T(512)} %param.22) | copy-start | bytes 6148
  25.3 3.8 %copy-start.1 = (bf16[32,128,576]{1,2,0:T(8,128)(2,1)S(1)}, bf16[32,128,576]{1,2,0:T(8,128)(2,1)}, u32[]{:S(2)}) copy-start(bf16[32,128,576]{1,2,0:T(8,128)(2,1)} %param.26) | copy-start | bytes 14155780
  29.1 1.2 copy-start.6
  29.1 1.8 copy-start.3
  30.3 1.7 copy-start.11
  30.3 2.1 %copy-start.7 = (s32[32,6]{0,1:T(8,128)S(1)}, s32[32,6]{0,1:T(8,128)}, u32[]{:S(2)}) copy-start(s32[32,6]{0,1:T(8,128)} %param.31) | copy-start | bytes 2308
  30.3 45.4 %copy-start.2 = (bf16[32,2048]{1,0:T(8,128)(2,1)S(1)}, bf16[32,2048]{1,0:T(8,128)(2,1)}, u32[]{:S(2)}) copy-start(bf16[32,2048]{1,0:T(8,128)(2,1)} %param.18) | copy-start | bytes 393220
  30.3 47.1 %copy-start.8 = (f32[2048]{0:T(1024)S(1)}, f32[2048]{0:T(1024)}, u32[]{:S(2)}) copy-start(f32[2048]{0:T(1024)} %param.29) | copy-start | bytes 24580
  32.0 120.0 %reduce-scatter.5.cloned.1.call-start = ((), (), s32[]{:S(2)}) async-start(), calls=%async_computation.6 | async-start | bytes 1966080 | tf_op jit(solution)/shard_map/reduce_scatter | solution.py:160
  76.8 0.6 copy-start.5
  122.4 5.9 %copy-start.10 = (bf16[2,352,2048]{2,1,0:T(8,128)(2,1)S(1)}, bf16[2,352,2048]{2,1,0:T(8,128)(2,1)}, u32[]{:S(2)}) copy-start(bf16[2,352,2048]{2,1,0:T(8,128)(2,1)} %param.33) | copy-start | bytes 8650756
  130.4 49.3 %reduce-scatter.3.cloned.1.call-start = ((), (), s32[]{:S(2)}) async-start(), calls=%async_computation.5 | async-start | bytes 163840 | tf_op jit(solution)/shard_map/reduce_scatter | solution.py:181
  134.3 3.0 %copy-start.4 = (bf16[352,2048]{1,0:T(8,128)(2,1)S(1)}, bf16[352,2048]{1,0:T(8,128)(2,1)}, u32[]{:S(2)}) copy-start(bf16[352,2048]{1,0:T(8,128)(2,1)} %param.35) | copy-start | bytes 4325380
  154.1 18.7 %all-to-all-start.1 = ((bf16[32,2,6,512]{3,1,2,0:T(2,128)(2,1)}), bf16[32,2,6,512]{3,1,2,0:T(2,128)(2,1)S(1)}, u32[]{:S(2)}, u32[]{:S(2)}) async-start(bf16[32,2,6,512]{3,1,2,0:T(2,128)(2,1)} %copy.99), calls=%async_computation.3 | async-start | bytes 786432 | tf_op jit(solution)/shard_map/all_to_all | solution.py:163
Sparse Core Ops, SparseCore 0:
  32.1 43.5 all-reduce.2
  130.6 21.3 reduce-scatter.4
  154.4 19.3 reduce-scatter.2
where the time goes:
time: 188 us
  waiting for transfers between devices  64.4 us (34%)
  blocking collectives  42.7 us (23%)
  local copies, waits for them, and re-layouts  25.4 us (14%)
  matrix products  23.6 us (13%)
  between operations  13.4 us (7%)
  other arithmetic  9.43 us (5%)
  starting transfers between devices  8.64 us (5%)
    psum x1, waiting for transfers between devices, body(): lax.psum(partial_value.astype(jnp.bfloat16), 'head').astype(jnp.float32)  41.9 us
    all_to_all x1, blocking collectives, body(): lax.all_to_all(packed.reshape(dp_count, local_experts, capacity, ffn_inpu...  32.3 us
    reduce_scatter x1, waiting for transfers between devices, body(): lax.psum_scatter(expert_part.astype(jnp.bfloat16), 'head', scatter_dimens...  13.7 us
    all_gather x1, blocking collectives, body(): fresh_kv = lax.all_gather(fresh_part, 'head', axis=1, tiled=True)  10.4 us
    all_to_all x1, waiting for transfers between devices, body(): lax.all_to_all(expert_share, 'dp', split_axis=0, concat_axis=0, tiled=True)  8.77 us
    all_to_all x1, starting transfers between devices, body(): lax.all_to_all(expert_share, 'dp', split_axis=0, concat_axis=0, tiled=True)  8.56 us
    reshape x2, local copies, waits for them, and re-layouts, body(): packed.reshape(dp_count, local_experts, capacity, ffn_input.shape[1])  6.93 us
    dot_general x1, matrix products, body(): jnp.einsum('secd,edkf->seckf', arrived, w_experts_in, preferred_element_t...  5.86 us
  transfers between devices with their start and end apart: 4, of which 3 were waited for; matrix products, arithmetic and copies ran while one was open for 11% of the time, Pallas kernels for 0%

commit v1 on v0

--- a/solution.py
+++ b/solution.py
@@ -11,6 +11,12 @@
 norm_eps = 1e-06
 rope_theta = 50000.0
 route_scale = 2.446
+
+
+def push_slots(z, link_axis):
+    return jnp.concatenate(
+        lax.all_to_all(jnp.stack([z] * lax.psum(1, link_axis), axis=0), link_axis, 0, 0), axis=1
+    )
 
 
 def rms_norm(values, weights):
@@ -78,7 +84,7 @@
         "rhn,hnc->rhc", query_nope, w_key_up, preferred_element_type=jnp.float32
     ).astype(jnp.bfloat16)
     fresh_part = jnp.dot(normed, w_latent, preferred_element_type=jnp.float32).astype(jnp.bfloat16)
-    fresh_kv = lax.all_gather(fresh_part, "head", axis=1, tiled=True)
+    fresh_kv = push_slots(fresh_part, "head")
     latent_new = rms_norm(fresh_kv[:, :LAT].astype(jnp.float32), latent_gain)
     rope_new = rotary(fresh_kv[:, LAT:].astype(jnp.float32), positions)
     key_new = jnp.concatenate([latent_new, rope_new], axis=-1).astype(jnp.bfloat16)

time: 188 us -> 187 us (level)
  blocking collectives: 42.7 us -> 32.3 us
  starting transfers between devices: 8.64 us -> 13.7 us
  local copies, waits for them, and re-layouts: 25.4 us -> 28.3 us
    all_gather x1 -> x0, blocking collectives: 10.4 us -> none  [body(): fresh_kv = lax.all_gather(fresh_part, 'head', axis=1, tiled=True)]
    all_to_all x0 -> x1, starting transfers between devices: none -> 5.01 us  [push_slots(): lax.all_to_all(jnp.stack([z] * lax.psum(1, link_axis), axis=0), link_axis...]
  transfers between devices with their start and end apart: 4 -> 5, of which waited for: 3 -> 3; matrix products, arithmetic and copies ran while one was open for 11% -> 14% of each run, Pallas kernels for 0% -> 0%
where the time goes in v1:
time: 187 us; the launch traced here: 186 us
  waiting for transfers between devices  64.7 us (35%)
  blocking collectives  32.3 us (17%)
  local copies, waits for them, and re-layouts  28.3 us (15%)
  matrix products  23.6 us (13%)
  starting transfers between devices  13.7 us (7%)
  between operations  13.4 us (7%)
  other arithmetic  9.97 us (5%)
    psum x1, waiting for transfers between devices, body(): lax.psum(partial_value.astype(jnp.bfloat16), 'head').astype(jnp.float32)  42.2 us
    all_to_all x1, blocking collectives, body(): lax.all_to_all(packed.reshape(dp_count, local_experts, capacity, ffn_inpu...  32.3 us
    reduce_scatter x1, waiting for transfers between devices, body(): lax.psum_scatter(expert_part.astype(jnp.bfloat16), 'head', scatter_dimens...  13.6 us
    all_to_all x1, waiting for transfers between devices, body(): lax.all_to_all(expert_share, 'dp', split_axis=0, concat_axis=0, tiled=True)  8.77 us
    all_to_all x1, starting transfers between devices, body(): lax.all_to_all(expert_share, 'dp', split_axis=0, concat_axis=0, tiled=True)  8.56 us
    reshape x2, local copies, waits for them, and re-layouts, body(): packed.reshape(dp_count, local_experts, capacity, ffn_input.shape[1])  6.93 us
    dot_general x1, matrix products, body(): jnp.einsum('secd,edkf->seckf', arrived, w_experts_in, preferred_element_t...  5.86 us
    scatter x1, local copies, waits for them, and re-layouts, body(): packed = jnp.zeros((slot_total, ffn_input.shape[1]), jnp.bfloat16).at[buf...  5.57 us
  transfers between devices with their start and end apart: 5, of which 3 were waited for; matrix products, arithmetic and copies ran while one was open for 14% of the time, Pallas kernels for 0%

profile of v1, /device:TPU:1, one launch (start us, length us, event | category | flops | bytes accessed | tf_op | source)
XLA Modules:
  0.0 186.0 jit_solution(16319379346289613200)
XLA Ops:
  6.5 1.2 fusion.39
  7.7 1.5 convolution_convert_fusion.4
  9.2 0.6 stack.2
  9.9 5.0 %all-to-all-start = ((bf16[4,32,144]{2,1,0:T(8,128)(2,1)}), bf16[4,32,144]{2,1,0:T(8,128)(2,1)S(1)}, u32[]{:S(2)}, u32[]{:S(2)}) async-start(bf16[4,32,144]{2,1,0:T(8,128)(2,1)} %stack.2), calls=%async_computation | async-start | bytes 131072 | tf_op jit(solution)/shard_map/all_to_all | solution.py:18
  14.9 0.7 broadcast_compare_fusion
  15.6 0.1 eq.62
  15.7 0.1 eq.57
  15.9 0.7 broadcast_multiply_fusion
  16.5 0.8 copy.109
  17.3 1.6 fusion.60
  18.9 0.1 reshape.319
  19.1 0.1 fusion.76
  19.3 0.1 copy.108
  19.4 0.1 mul.265
  19.5 0.1 eq.58
  19.6 0.6 reduce-window.6
  20.2 0.2 slice_reduce_fusion
  20.5 0.1 bitcast_bitcast_fusion
  20.6 1.2 fusion.26
  21.9 0.7 convert_element_type.107
  22.5 0.7 copy.101
  23.2 1.0 reshape.321
  24.2 0.1 fusion.49
  24.4 0.1 subtract_convert_fusion.1
  24.5 0.1 maximum_bitcast_fusion
  24.6 0.1 pad_maximum_fusion
  24.7 0.3 fusion.45
  25.0 3.4 %fusion.77 = (f32[32,4]{1,0:T(8,128)S(1)}, f32[32,4,128]{2,1,0:T(4,128)S(1)}) fusion(bf16[32,128,576]{1,2,0:T(8,128)(2,1)} %param.26, bf16[32,4,576]{2,0,1:T(8,128)(2,1)S(1)} %pad_maximum_fusion, pred[32,128]{1,0:T(8,128)(4,1)S(1)} %iota_compare_fusion.2), kind=kOutput, calls=%fused_computation.127 | convolution fusion | flops 18923392 | bytes 4936192 | tf_op jit(solution)/shard_map/rhc,rjc->rhj/dot_general | solution.py:94
  28.4 0.2 fusion.56
  28.6 0.1 copy-done.1
  28.8 1.2 fusion.23
  30.0 0.2 fusion.28
  30.3 0.3 copy-done.3
  30.6 1.1 convolution_convert_fusion.1
  31.8 42.2 %all-reduce.3.cloned.1.call-done = bf16[32,2048]{1,0:T(8,128)(2,1)} async-done(((bf16[32,2048]{1,0:T(8,128)(2,1)}), bf16[32,2048]{1,0:T(8,128)(2,1)}) %all-reduce.3.cloned.1.call-update) | async-done | bytes 131088 | tf_op jit(solution)/shard_map/psum | solution.py:122
  74.0 1.1 fusion.36
  75.0 0.6 copy-done.5
  75.7 0.1 fusion.38
  75.8 5.6 %scatter_custom_fusion = bf16[384,2048]{1,0:T(8,128)(2,1)} fusion(s32[192]{0:T(256)S(1)} %bitcast.106, bf16[32,2048]{1,0:T(8,128)(2,1)S(1)} %fusion.38, s32[1024]{0:T(1024)S(1)} %pad_clamp_fusion.1, bf16[]{:T(256)} %constant.75.clone.1), kind=kCustom, calls=%fused_computation.27 | custom fusion | bytes 1572866 | tf_op jit(solution)/shard_map/scatter | solution.py:150
  81.3 3.7 %reshape.327 = bf16[32,2,6,2048]{3,2,1,0:T(8,128)(2,1)} reshape(bf16[384,2048]{1,0:T(8,128)(2,1)} %scatter_custom_fusion) | data formatting | bytes 3145728 | tf_op jit(solution)/shard_map/reshape | solution.py:153
  85.1 3.2 %copy.112 = bf16[32,2,6,2048]{3,1,2,0:T(2,128)(2,1)S(1)} copy(bf16[32,2,6,2048]{3,2,1,0:T(8,128)(2,1)} %reshape.327) | data formatting | bytes 3145728 | tf_op jit(solution)/shard_map/reshape | solution.py:153
  88.3 32.3 %all_to_all.15 = bf16[32,2,6,2048]{3,1,2,0:T(2,128)(2,1)S(1)} all-to-all(bf16[32,2,6,2048]{3,1,2,0:T(2,128)(2,1)S(1)} %copy.112), channel_id=1, replica_groups=mesh['dp'=32,'head'=4] {'dp'}, dimensions={0} | all-to-all | bytes 3145728 | tf_op jit(solution)/shard_map/all_to_all | solution.py:152
  120.6 5.9 %fusion.15 = f32[32,2,6,2,352]{4,0,3,2,1:T(8,128)S(1)} fusion(bf16[2,2048,2,352]{1,3,2,0:T(8,128)(2,1)} %param.32, bf16[32,2,6,2048,1]{3,1,2,0,4:T(2,128)(2,1)S(1)} %bitcast.100), kind=kOutput, calls=%fused_computation.17 | convolution fusion | flops 1107296256 | bytes 8421376 | tf_op jit(solution)/shard_map/secd,edkf->seckf/dot_general | solution.py:159
  126.5 2.2 %fusion.11 = bf16[32,2,6,2048]{3,0,2,1:T(8,128)(2,1)} fusion(bf16[2,352,2048]{2,1,0:T(8,128)(2,1)S(1)} %copy-done.11, f32[32,2,6,2,352]{4,0,3,2,1:T(8,128)S(1)} %fusion.15), kind=kOutput, calls=%fused_computation.13 | convolution fusion | flops 555245568 | bytes 5537792 | tf_op jit(solution)/shard_map/secf,efd->secd/dot_general | solution.py:163
  128.8 0.1 copy.105
  128.9 0.1 reshape.347
  129.0 0.6 pad_clamp_fusion
  129.6 1.1 fusion.78
  130.7 1.6 gather_fusion.1
  132.4 0.1 reshape.350
  132.5 2.9 %fusion.6 = f32[32,2,352]{2,0,1:T(8,128)S(1)} fusion(bf16[2048,2,352]{0,2,1:T(8,128)(2,1)} %param.34, bf16[32,2048]{1,0:T(8,128)(2,1)S(1)} %fusion.38), kind=kOutput, calls=%fused_computation.10 | convolution fusion | flops 92274688 | bytes 3104768 | tf_op jit(solution)/shard_map/dot_general | solution.py:180
  135.5 1.0 convolution_convert_fusion
  136.6 13.6 %reduce-scatter.5.cloned.1.call-done = bf16[32,2,6,512]{3,0,2,1:T(8,128)(2,1)} async-done(((bf16[32,2,6,2048]{3,0,2,1:T(8,128)(2,1)}), bf16[32,2,6,512]{3,0,2,1:T(8,128)(2,1)}) %reduce-scatter.5.cloned.1.call-update) | async-done | bytes 393232 | tf_op jit(solution)/shard_map/reduce_scatter | solution.py:166
  150.2 2.1 %copy.115 = bf16[32,2,6,512]{3,1,2,0:T(2,128)(2,1)} copy(bf16[32,2,6,512]{3,0,2,1:T(8,128)(2,1)} %reduce-scatter.5.cloned.1.call-done) | data formatting | bytes 786432 | tf_op jit(solution)/shard_map/reduce_scatter | solution.py:166
  152.3 8.6 %all-to-all-start.2 = ((bf16[32,2,6,512]{3,1,2,0:T(2,128)(2,1)}), bf16[32,2,6,512]{3,1,2,0:T(2,128)(2,1)S(1)}, u32[]{:S(2)}, u32[]{:S(2)}) async-start(bf16[32,2,6,512]{3,1,2,0:T(2,128)(2,1)} %copy.115), calls=%async_computation.4 | async-start | bytes 786432 | tf_op jit(solution)/shard_map/all_to_all | solution.py:169
  160.9 0.6 multiply_divide_fusion
  161.5 0.8 copy.107
  162.3 8.8 %all-to-all-done.2 = bf16[32,2,6,512]{3,1,2,0:T(2,128)(2,1)S(1)} async-done(((bf16[32,2,6,512]{3,1,2,0:T(2,128)(2,1)}), bf16[32,2,6,512]{3,1,2,0:T(2,128)(2,1)S(1)}, u32[]{:S(2)}, u32[]{:S(2)}) %all-to-all-start.2) | async-done | bytes 393248 | tf_op jit(solution)/shard_map/all_to_all | solution.py:169
  171.1 0.9 copy.116
  172.0 1.2 reshape.328
  173.1 1.8 gather_fusion
  174.9 1.8 reshape.330
  176.7 1.3 multiply_reduce_fusion
  178.0 1.4 add_convert_fusion
  (55 shorter events, 0.8 us)
Async XLA Ops:
  6.5 10.8 %copy-start = (bf16[2048,768]{1,0:T(8,128)(2,1)S(1)}, bf16[2048,768]{1,0:T(8,128)(2,1)}, u32[]{:S(2)}) copy-start(bf16[2048,768]{1,0:T(8,128)(2,1)} %param.20) | copy-start | bytes 9437188
  9.2 10.0 %copy-start.10 = (s32[32]{0:T(128)S(1)}, s32[32]{0:T(128)}, u32[]{:S(2)}) copy-start(s32[32]{0:T(128)} %param.27) | copy-start | bytes 388
  9.9 12.7 %all-to-all-start = ((bf16[4,32,144]{2,1,0:T(8,128)(2,1)}), bf16[4,32,144]{2,1,0:T(8,128)(2,1)S(1)}, u32[]{:S(2)}, u32[]{:S(2)}) async-start(bf16[4,32,144]{2,1,0:T(8,128)(2,1)} %stack.2), calls=%async_computation | async-start | bytes 131072 | tf_op jit(solution)/shard_map/all_to_all | solution.py:18
  14.9 59.1 %all-reduce.3.cloned.1.call-start = ((), (), s32[]{:S(2)}) async-start(), calls=%async_computation.5 | async-start | bytes 262144 | tf_op jit(solution)/shard_map/psum | solution.py:122
  17.3 7.0 %copy-start.9 = (f32[512]{0:T(512)S(1)}, f32[512]{0:T(512)}, u32[]{:S(2)}) copy-start(f32[512]{0:T(512)} %param.22) | copy-start | bytes 6148
  25.0 3.8 %copy-start.1 = (bf16[32,128,576]{1,2,0:T(8,128)(2,1)S(1)}, bf16[32,128,576]{1,2,0:T(8,128)(2,1)}, u32[]{:S(2)}) copy-start(bf16[32,128,576]{1,2,0:T(8,128)(2,1)} %param.26) | copy-start | bytes 14155780
  28.8 1.2 copy-start.6
  28.8 1.8 copy-start.3
  30.0 43.9 %copy-start.2 = (bf16[32,2048]{1,0:T(8,128)(2,1)S(1)}, bf16[32,2048]{1,0:T(8,128)(2,1)}, u32[]{:S(2)}) copy-start(bf16[32,2048]{1,0:T(8,128)(2,1)} %param.18) | copy-start | bytes 393220
  30.0 45.6 %copy-start.8 = (f32[2048]{0:T(1024)S(1)}, f32[2048]{0:T(1024)}, u32[]{:S(2)}) copy-start(f32[2048]{0:T(1024)} %param.29) | copy-start | bytes 24580
  31.7 118.5 %reduce-scatter.5.cloned.1.call-start = ((), (), s32[]{:S(2)}) async-start(), calls=%async_computation.7 | async-start | bytes 1966080 | tf_op jit(solution)/shard_map/reduce_scatter | solution.py:166
  75.0 0.6 copy-start.5
  120.6 5.9 %copy-start.11 = (bf16[2,352,2048]{2,1,0:T(8,128)(2,1)S(1)}, bf16[2,352,2048]{2,1,0:T(8,128)(2,1)}, u32[]{:S(2)}) copy-start(bf16[2,352,2048]{2,1,0:T(8,128)(2,1)} %param.33) | copy-start | bytes 8650756
  126.5 2.3 %copy-start.7 = (s32[32,6]{0,1:T(8,128)S(1)}, s32[32,6]{0,1:T(8,128)}, u32[]{:S(2)}) copy-start(s32[32,6]{0,1:T(8,128)} %param.31) | copy-start | bytes 2308
  126.5 3.1 %copy-start.12 = (s32[32]{0:T(128)S(1)}, s32[32]{0:T(128)}, u32[]{:S(2)}) copy-start(s32[32]{0:T(128)} %param.28) | copy-start | bytes 388
  128.7 49.3 %reduce-scatter.3.cloned.1.call-start = ((), (), s32[]{:S(2)}) async-start(), calls=%async_computation.6 | async-start | bytes 163840 | tf_op jit(solution)/shard_map/reduce_scatter | solution.py:187
  132.5 3.0 %copy-start.4 = (bf16[352,2048]{1,0:T(8,128)(2,1)S(1)}, bf16[352,2048]{1,0:T(8,128)(2,1)}, u32[]{:S(2)}) copy-start(bf16[352,2048]{1,0:T(8,128)(2,1)} %param.35) | copy-start | bytes 4325380
  152.3 18.7 %all-to-all-start.2 = ((bf16[32,2,6,512]{3,1,2,0:T(2,128)(2,1)}), bf16[32,2,6,512]{3,1,2,0:T(2,128)(2,1)S(1)}, u32[]{:S(2)}, u32[]{:S(2)}) async-start(bf16[32,2,6,512]{3,1,2,0:T(2,128)(2,1)} %copy.115), calls=%async_computation.4 | async-start | bytes 786432 | tf_op jit(solution)/shard_map/all_to_all | solution.py:169
Sparse Core Ops, SparseCore 0:
  31.8 42.0 all-reduce.2
  128.8 21.3 reduce-scatter.4
  152.7 19.3 reduce-scatter.2
